TPU v7x, 32 devices: a whole 2x2x4 slice. The times are simulated.
32 devices in a mesh: shard: 2 (over y), ctx: 4 (over x, core), tp: 4 (over z).
Axes of the slice: x: 2, y: 2, z: 4, core: 2. Of those that a mesh axis runs over, the one named last changes fastest.
Arguments:
- tokens: bfloat16 [2, 2, 2560, 1280], P(None, 'shard', ('ctx', 'tp')), may hold values from -0.16992188 to 0.16992188
- parents: int32 [2, 2, 40], P(None, 'shard'), may hold values from 0 to 38, as said below
- slot_segment: int32 [2, 2, 40], P(None, 'shard'), may hold values from 0 to 39, each once within a row
- w_query: bfloat16 [1280, 1280], P(('shard', 'ctx'), 'tp'), may hold values from -0.15625 to 0.15625
- w_key: bfloat16 [1280, 1280], P(('shard', 'ctx'), 'tp'), may hold values from -0.15625 to 0.15625
- w_value: bfloat16 [1280, 1280], P(('shard', 'ctx'), 'tp'), may hold values from -0.15625 to 0.15625
- w_attn_out: bfloat16 [1280, 1280], P('tp', ('shard', 'ctx')), may hold values from -0.15625 to 0.15625
- w_up: bfloat16 [1280, 5120], P(('shard', 'ctx'), 'tp'), may hold values from -0.15625 to 0.15625
- w_gate: bfloat16 [1280, 5120], P(('shard', 'ctx'), 'tp'), may hold values from -0.15625 to 0.15625
- w_down: bfloat16 [5120, 1280], P('tp', ('shard', 'ctx')), may hold values from -0.078125 to 0.078125
- alpha_attn: float32 [1280], replicated, may hold values from 0.15 to 0.6
- alpha_mlp: float32 [1280], replicated, may hold values from 0.15 to 0.6
- scale_qk: float32 [1280], P('tp'), may hold values from 0.7 to 1.4
- scale_up: float32 [5120], P('tp'), may hold values from 0.5 to 2
- scale_gate: float32 [5120], P('tp'), may hold values from 0.5 to 2
- cotangent: bfloat16 [2, 2, 2560, 1280], P(None, 'shard', ('ctx', 'tp')), may hold values from -6 to 6
Outputs:
- block_out: bfloat16 [2, 2, 2560, 1280], P(None, 'shard', ('ctx', 'tp'))
- grad_tokens: float32 [2, 2, 2560, 1280], P(None, 'shard', ('ctx', 'tp'))
- grad_w_query: float32 [1280, 1280], P(('shard', 'ctx'), 'tp')
- grad_w_key: float32 [1280, 1280], P(('shard', 'ctx'), 'tp')
- grad_w_value: float32 [1280, 1280], P(('shard', 'ctx'), 'tp')
- grad_w_attn_out: float32 [1280, 1280], P('tp', ('shard', 'ctx'))
- grad_w_up: float32 [1280, 5120], P(('shard', 'ctx'), 'tp')
- grad_w_gate: float32 [1280, 5120], P(('shard', 'ctx'), 'tp')
- grad_w_down: float32 [5120, 1280], P('tp', ('shard', 'ctx'))
- grad_alpha_attn: float32 [1280], replicated
- grad_alpha_mlp: float32 [1280], replicated
- grad_scale_qk: float32 [1280], P('tp')
- grad_scale_up: float32 [5120], P('tp')
- grad_scale_gate: float32 [5120], P('tp')
Inputs may be any that keep to these rules, and one draw needn't show every extreme that they name: `parents`: segment 0 of each tree is its root and names itself; every other segment names a segment with a lower number; every segment has 64 tokens. `slot_segment`: each tree's 40 slots hold its segments, each once.
All inputs are finite; a program needn't handle non-finite values.
Results may differ from a plain program's by a relative error of at most 0.019.
Values may be sent and summed in bfloat16 or wider, within the bound.
No kernel may reach another device: no remote copies, remote signals or barrier semaphores. Data moves between devices by JAX's collectives and lax.ppermute only.
A program may use at most 120 MiB of HBM per device.

v0:
```python
import math
import jax
import jax.numpy as jnp
from jax import lax
from jax.sharding import PartitionSpec as P

D = 1280
HDIM = 64
SEG = 64
SEGS = 40
TREE_TOK = 2560
EPSILON = 1e-06
MASKED = -1e30
HIGHEST = lax.Precision.HIGHEST


def unit_rows(values):
    return values * lax.rsqrt(jnp.sum(values * values, axis=-1, keepdims=True) + EPSILON)


def unit_heads(values):
    shaped = values.reshape(values.shape[0], values.shape[1] // HDIM, HDIM)
    return unit_rows(shaped).reshape(values.shape)


def contract_rows(former, latter):
    return lax.dot_general(
        former, latter, (((0,), (0,)), ((), ())), preferred_element_type=jnp.float32
    )


def contract_cols(former, latter):
    return lax.dot_general(
        former, latter, (((1,), (1,)), ((), ())), preferred_element_type=jnp.float32
    )


def split_heads(values):
    return values.reshape(values.shape[0], values.shape[1] // HDIM, HDIM).transpose(1, 0, 2)


def merge_heads(values):
    return values.transpose(1, 0, 2).reshape(values.shape[1], values.shape[0] * values.shape[2])


def mix_rows(residual, branch, mixing):
    return unit_rows(residual + mixing * (unit_rows(branch) - residual))


def query_key(query_raw, key_raw, gain_qk):
    return (unit_heads(query_raw) * gain_qk, unit_heads(key_raw) * gain_qk)


def middle(up_raw, gate_raw, scale_up, scale_gate):
    return up_raw * scale_up * jax.nn.silu(gate_raw * (scale_gate * math.sqrt(D)))


def group_rows(own_block):
    return lax.all_gather(own_block, "tp", axis=0, tiled=True)


def group_grads(own_block):
    return lax.all_gather(own_block, "tp", axis=0, tiled=True)


def own_rows(partial_value):
    return own_grads(partial_value)


def own_grads(partial_value):
    return lax.psum_scatter(
        partial_value.astype(jnp.bfloat16), "tp", scatter_dimension=0, tiled=True
    ).astype(jnp.float32)


def visibility(parents, slots, group_size):
    labels = jnp.arange(SEGS, dtype=jnp.int32)
    linked = (parents[:, None] == labels[None, :]).astype(jnp.float32)
    reachable = jnp.maximum(linked, jnp.eye(SEGS, dtype=jnp.float32))
    for doubling in range(SEGS.bit_length()):
        reachable = jnp.minimum(jnp.dot(reachable, reachable, precision=HIGHEST), 1.0)
    segment = jnp.broadcast_to(slots[:, None], (SEGS, SEG)).reshape(TREE_TOK)
    offset = lax.broadcasted_iota(jnp.int32, (SEGS, SEG), 1).reshape(TREE_TOK)
    first_row = lax.axis_index("ctx") * group_size
    seg_query = lax.dynamic_slice_in_dim(segment, first_row, group_size)
    off_query = lax.dynamic_slice_in_dim(offset, first_row, group_size)
    key_onehot = (segment[:, None] == labels[None, :]).astype(jnp.float32)
    query_onehot = (seg_query[:, None] == labels[None, :]).astype(jnp.float32)
    linked_rows = jnp.dot(query_onehot, reachable, precision=HIGHEST)
    seen = (
        lax.dot_general(linked_rows, key_onehot, (((1,), (1,)), ((), ())), precision=HIGHEST) > 0.5
    )
    return seen & (
        (seg_query[:, None] != segment[None, :]) | (offset[None, :] <= off_query[:, None])
    )


def forward_attention(gathered, vectors, tokens_own, parents, slots):
    w_query, w_key, w_value, w_attn_out = gathered[:4]
    alpha_attn, alpha_mlp, scale_qk, scale_up, scale_gate = vectors
    score_scale = math.sqrt(HDIM)
    hidden_group = group_rows(tokens_own)
    visible = visibility(parents, slots, hidden_group.shape[0])
    query_raw = jnp.dot(hidden_group, w_query, preferred_element_type=jnp.float32)
    key_raw = jnp.dot(hidden_group, w_key, preferred_element_type=jnp.float32)
    value_low = jnp.dot(hidden_group, w_value, preferred_element_type=jnp.float32).astype(
        jnp.bfloat16
    )
    query_unit, key_unit = query_key(query_raw, key_raw, scale_qk)
    queries = query_unit.astype(jnp.bfloat16)
    keys_own = key_unit.astype(jnp.bfloat16)
    keys_values = lax.all_gather(
        jnp.concatenate([keys_own, value_low], axis=1), "ctx", axis=0, tiled=True
    )
    keys_tree, values_tree = jnp.split(keys_values, 2, axis=1)
    query_heads = split_heads(queries)
    key_heads = split_heads(keys_tree)
    value_heads = split_heads(values_tree)

    def head_forward(record):
        query_one, key_one, value_one = record
        scores = jnp.where(visible, contract_cols(query_one, key_one) * score_scale, MASKED)
        row_peak = jnp.max(scores, axis=-1, keepdims=True)
        lifted = jnp.exp(scores - row_peak)
        row_total = jnp.sum(lifted, axis=-1, keepdims=True)
        soft_weights = lifted / row_total
        head_value = jnp.dot(
            soft_weights.astype(jnp.bfloat16), value_one, preferred_element_type=jnp.float32
        )
        return (head_value, (row_peak + jnp.log(row_total))[:, 0])

    head_values, log_totals = lax.map(head_forward, (query_heads, key_heads, value_heads))
    heads_low = merge_heads(head_values).astype(jnp.bfloat16)
    branch_one = own_rows(jnp.dot(heads_low, w_attn_out, preferred_element_type=jnp.float32))
    kept = (
        hidden_group,
        visible,
        query_raw,
        key_raw,
        query_heads,
        key_heads,
        value_heads,
        log_totals,
        heads_low,
    )
    return (branch_one, kept)


def feed_forward(gathered, vectors, tokens_own, branch_one, cotangent_own):
    w_up, w_gate, w_down = gathered[4:]
    alpha_attn, alpha_mlp, scale_qk, scale_up, scale_gate = vectors
    tokens_wide = tokens_own.astype(jnp.float32)
    hidden_one = mix_rows(tokens_wide, branch_one, alpha_attn)
    hidden_one_group = group_rows(hidden_one.astype(jnp.bfloat16))
    up_raw = jnp.dot(hidden_one_group, w_up, preferred_element_type=jnp.float32)
    gate_raw = jnp.dot(hidden_one_group, w_gate, preferred_element_type=jnp.float32)
    mixed_low = middle(up_raw, gate_raw, scale_up, scale_gate).astype(jnp.bfloat16)
    branch_two = own_rows(jnp.dot(mixed_low, w_down, preferred_element_type=jnp.float32))
    output_wide, pull_out = jax.vjp(mix_rows, hidden_one, branch_two, alpha_mlp)
    upstream = cotangent_own.astype(jnp.float32)
    hidden_one_direct, branch_two_grad, grad_alpha_mlp = pull_out(upstream)
    branch_two_group = group_grads(branch_two_grad.astype(jnp.bfloat16))
    mixed_grad = contract_cols(branch_two_group, w_down).astype(jnp.bfloat16).astype(jnp.float32)
    middle_value, pull_mid = jax.vjp(middle, up_raw, gate_raw, scale_up, scale_gate)
    up_grad, gate_grad, grad_scale_up, grad_scale_gate = pull_mid(mixed_grad)
    up_low = up_grad.astype(jnp.bfloat16)
    gate_low = gate_grad.astype(jnp.bfloat16)
    hidden_one_grad = hidden_one_direct + own_grads(
        contract_cols(up_low, w_up) + contract_cols(gate_low, w_gate)
    )
    hidden_again, pull_in = jax.vjp(mix_rows, tokens_wide, branch_one, alpha_attn)
    tokens_direct, branch_one_grad, grad_alpha_attn = pull_in(hidden_one_grad)
    factors = (mixed_low, branch_two_group, hidden_one_group, up_low, gate_low)
    sums = (grad_alpha_attn, grad_alpha_mlp, grad_scale_up, grad_scale_gate)
    return (output_wide.astype(jnp.bfloat16), tokens_direct, branch_one_grad, factors, sums)


def backward_attention(gathered, vectors, kept, branch_one_grad, tokens_direct):
    w_query, w_key, w_value, w_attn_out = gathered[:4]
    scale_qk = vectors[2]
    score_scale = math.sqrt(HDIM)
    (
        hidden_group,
        visible,
        query_raw,
        key_raw,
        query_heads,
        key_heads,
        value_heads,
        log_totals,
        heads_low,
    ) = kept
    branch_one_group = group_grads(branch_one_grad.astype(jnp.bfloat16))
    heads_grad = split_heads(contract_cols(branch_one_group, w_attn_out).astype(jnp.bfloat16))

    def head_backward(record):
        query_one, key_one, value_one, upstream_one, log_total = record
        scores = jnp.where(visible, contract_cols(query_one, key_one) * score_scale, MASKED)
        soft_weights = jnp.exp(scores - log_total[:, None])
        weight_grad = contract_cols(upstream_one, value_one)
        row_inner = jnp.sum(soft_weights * weight_grad, axis=-1, keepdims=True)
        score_grad = (soft_weights * (weight_grad - row_inner)).astype(jnp.bfloat16)
        query_grad = jnp.dot(score_grad, key_one, preferred_element_type=jnp.float32) * score_scale
        key_grad = contract_rows(score_grad, query_one) * score_scale
        value_grad = contract_rows(soft_weights.astype(jnp.bfloat16), upstream_one)
        return (query_grad, key_grad, value_grad)

    query_grads, key_grads, value_grads = lax.map(
        head_backward, (query_heads, key_heads, value_heads, heads_grad, log_totals)
    )
    both = lax.psum_scatter(
        jnp.concatenate([merge_heads(key_grads), merge_heads(value_grads)], axis=1).astype(
            jnp.bfloat16
        ),
        "ctx",
        scatter_dimension=0,
        tiled=True,
    ).astype(jnp.float32)
    key_own_grad, value_own_grad = jnp.split(both, 2, axis=1)
    unit_again, pull_qk = jax.vjp(query_key, query_raw, key_raw, scale_qk)
    query_raw_grad, key_raw_grad, grad_scale_qk = pull_qk((merge_heads(query_grads), key_own_grad))
    query_low = query_raw_grad.astype(jnp.bfloat16)
    key_low = key_raw_grad.astype(jnp.bfloat16)
    value_grad_low = value_own_grad.astype(jnp.bfloat16)
    input_part = (
        contract_cols(query_low, w_query)
        + contract_cols(key_low, w_key)
        + contract_cols(value_grad_low, w_value)
    )
    grad_tokens = tokens_direct + own_grads(input_part)
    factors = (hidden_group, query_low, key_low, value_grad_low, heads_low, branch_one_group)
    return (grad_tokens, factors, grad_scale_qk)


def per_device(
    tokens,
    parents,
    slot_segment,
    w_query,
    w_key,
    w_value,
    w_attn_out,
    w_up,
    w_gate,
    w_down,
    alpha_attn,
    alpha_mlp,
    scale_qk,
    scale_up,
    scale_gate,
    cotangent,
):
    local_heads = w_query.shape[1]
    local_hidden = w_up.shape[1]
    vectors = (alpha_attn, alpha_mlp, scale_qk, scale_up, scale_gate)
    spread = ("shard", "ctx")
    gathered = (
        lax.all_gather(w_query, spread, axis=0, tiled=True),
        lax.all_gather(w_key, spread, axis=0, tiled=True),
        lax.all_gather(w_value, spread, axis=0, tiled=True),
        lax.all_gather(w_attn_out, spread, axis=1, tiled=True),
        lax.all_gather(w_up, spread, axis=0, tiled=True),
        lax.all_gather(w_gate, spread, axis=0, tiled=True),
        lax.all_gather(w_down, spread, axis=1, tiled=True),
    )
    micros = range(tokens.shape[0])
    front = [
        forward_attention(gathered, vectors, tokens[m, 0], parents[m, 0], slot_segment[m, 0])
        for m in micros
    ]
    mid = [
        feed_forward(gathered, vectors, tokens[m, 0], front[m][0], cotangent[m, 0]) for m in micros
    ]
    back = [
        backward_attention(gathered, vectors, front[m][1], mid[m][2], mid[m][1]) for m in micros
    ]

    def stack(pick):
        return jnp.concatenate([pick(m) for m in micros], axis=0)

    mixed_all, top_all, hidden_all, up_all, gate_all = (
        stack(lambda m: mid[m][3][place]) for place in range(5)
    )
    tokens_all, query_all, key_all, value_all, heads_all, branch_all = (
        stack(lambda m: back[m][1][place]) for place in range(6)
    )

    def to_owner(former, latter, axis):
        product = contract_rows(former, latter).astype(jnp.bfloat16)
        return lax.psum_scatter(product, spread, scatter_dimension=axis, tiled=True).astype(
            jnp.float32
        )

    grad_d = to_owner(mixed_all, top_all, 1)
    grad_u = to_owner(hidden_all, up_all, 0)
    grad_g = to_owner(hidden_all, gate_all, 0)
    grad_o = to_owner(heads_all, branch_all, 1)
    grad_q = to_owner(tokens_all, query_all, 0)
    grad_k = to_owner(tokens_all, key_all, 0)
    grad_v = to_owner(tokens_all, value_all, 0)
    sum_attn, sum_mlp, sum_up, sum_gate = (
        sum((mid[m][4][place] for m in micros)) for place in range(4)
    )
    sum_qk = sum((back[m][2] for m in micros))
    tp_count = lax.axis_size("tp")
    tp_place = lax.axis_index("tp")

    def padded(vector):
        return lax.dynamic_update_slice_in_dim(
            jnp.zeros((vector.shape[0] * tp_count,), jnp.float32),
            vector,
            tp_place * vector.shape[0],
            0,
        )

    alpha_attn_sum, alpha_mlp_sum, qk_sum, up_sum, gate_sum = lax.psum(
        (sum_attn, sum_mlp, padded(sum_qk), padded(sum_up), padded(sum_gate)),
        ("shard", "ctx", "tp"),
    )
    return (
        jnp.stack([mid[m][0] for m in micros])[:, None],
        jnp.stack([back[m][0] for m in micros])[:, None],
        grad_q,
        grad_k,
        grad_v,
        grad_o,
        grad_u,
        grad_g,
        grad_d,
        alpha_attn_sum,
        alpha_mlp_sum,
        lax.dynamic_slice_in_dim(qk_sum, tp_place * local_heads, local_heads),
        lax.dynamic_slice_in_dim(up_sum, tp_place * local_hidden, local_hidden),
        lax.dynamic_slice_in_dim(gate_sum, tp_place * local_hidden, local_hidden),
    )


def solution(mesh):
    return jax.shard_map(
        per_device,
        mesh=mesh,
        in_specs=(
            P(None, "shard", ("ctx", "tp"), None),
            P(None, "shard", None),
            P(None, "shard", None),
            P(("shard", "ctx"), "tp"),
            P(("shard", "ctx"), "tp"),
            P(("shard", "ctx"), "tp"),
            P("tp", ("shard", "ctx")),
            P(("shard", "ctx"), "tp"),
            P(("shard", "ctx"), "tp"),
            P("tp", ("shard", "ctx")),
            P(),
            P(),
            P("tp"),
            P("tp"),
            P("tp"),
            P(None, "shard", ("ctx", "tp"), None),
        ),
        out_specs=(
            P(None, "shard", ("ctx", "tp"), None),
            P(None, "shard", ("ctx", "tp"), None),
            P(("shard", "ctx"), "tp"),
            P(("shard", "ctx"), "tp"),
            P(("shard", "ctx"), "tp"),
            P("tp", ("shard", "ctx")),
            P(("shard", "ctx"), "tp"),
            P(("shard", "ctx"), "tp"),
            P("tp", ("shard", "ctx")),
            P(),
            P(),
            P("tp"),
            P("tp"),
            P("tp"),
        ),
        check_vma=False,
    )
```

profile of v0, /device:TPU:0, one launch (start us, length us, event | category | flops | bytes accessed | tf_op | source)
XLA Modules:
  0.0 1370.7 jit_solution(1674269570403214196)
XLA Ops:
  11.0 14.3 %all_gather.52 = bf16[1280,320]{1,0:T(8,128)(2,1)} all-gather(bf16[160,320]{1,0:T(8,128)(2,1)} %param.27), channel_id=1, replica_groups=mesh['shard'=2,'ctx'=4,'tp'=4] {'shard','ctx'}, dimensions={0}, use_global_device_ids=true | all-gather | bytes 921600 | tf_op jit(solution)/shard_map/all_gather | solution.py:258
  25.3 10.2 all_gather.53
  35.4 12.0 all_gather.54
  54.6 36.5 %all-gather.38.cloned.1.call-done = bf16[1,1,640,1280]{3,2,1,0:T(8,128)(2,1)} async-done(((bf16[1,1,160,1280]{3,2,1,0:T(8,128)(2,1)}), bf16[1,1,640,1280]{3,2,1,0:T(8,128)(2,1)}) %all-gather.38.cloned.1.call-update) | async-done | bytes 1638416 | tf_op jit(solution)/shard_map/all_gather | solution.py:59
  109.7 15.2 %all_gather.56 = bf16[320,1280]{0,1:T(8,128)(2,1)} all-gather(bf16[320,160]{0,1:T(8,128)(2,1)S(1)} %copy-done.91), channel_id=1, replica_groups=mesh['shard'=2,'ctx'=4,'tp'=4] {'shard','ctx'}, dimensions={1}, use_global_device_ids=true | all-gather | bytes 921600 | tf_op jit(solution)/shard_map/all_gather | solution.py:261
  131.7 7.4 all-gather.16.cloned.1.call-done
  150.4 57.9 %while.52 = (s32[]{:T(128)}, bf16[5,640,64]{1,2,0:T(8,128)(2,1)}, f32[5,640]{1,0:T(8,128)}, bf16[5,640,64]{2,1,0:T(8,128)(2,1)}, bf16[5,2560,64]{2,1,0:T(8,128)(...) while((s32[]{:T(128)}, bf16[5,640,64]{1,2,0:T(8,128)(2,1)}, ...), condition=%wide.region_5.6_spmd, body=%wide.region_2.5_spmd.sunk | while | flops 432536960 | bytes 49184892 | solution.py:132
  180.2 4.9 fusion.305
  213.1 33.7 %reduce-scatter.22.cloned.1.call-done = bf16[160,1280]{1,0:T(8,128)(2,1)} async-done(((bf16[640,1280]{1,0:T(8,128)(2,1)}), bf16[160,1280]{1,0:T(8,128)(2,1)}) %reduce-scatter.22.cloned.1.call-update) | async-done | bytes 409616 | tf_op jit(solution)/shard_map/reduce_scatter | solution.py:71
  257.4 32.3 %all-gather.18.cloned.1.call-done = bf16[640,1280]{1,0:T(8,128)(2,1)} async-done(((bf16[160,1280]{1,0:T(8,128)(2,1)}), bf16[640,1280]{1,0:T(8,128)(2,1)}) %all-gather.18.cloned.1.call-update) | async-done | bytes 1638416 | tf_op jit(solution)/shard_map/all_gather | solution.py:59
  289.8 6.5 fusion.186
  296.3 27.0 %all-gather.20.cloned.1.call-done = bf16[1280,1280]{1,0:T(8,128)(2,1)} async-done(((bf16[160,1280]{1,0:T(8,128)(2,1)}), bf16[1280,1280]{1,0:T(8,128)(2,1)}) %all-gather.20.cloned.1.call-update) | async-done | bytes 3276816 | tf_op jit(solution)/shard_map/all_gather | solution.py:262
  323.3 7.6 multiply_convert_fusion.7
  330.9 27.2 %all-gather.24.cloned.1.call-done = bf16[1280,1280]{0,1:T(8,128)(2,1)} async-done(((bf16[1280,160]{0,1:T(8,128)(2,1)}), bf16[1280,1280]{0,1:T(8,128)(2,1)}) %all-gather.24.cloned.1.call-update) | async-done | bytes 3276816 | tf_op jit(solution)/shard_map/all_gather | solution.py:264
  358.0 5.9 convolution_convert_fusion.7
  371.1 17.7 %all-gather.26.cloned.1.call-done = bf16[2560,640]{0,1:T(8,128)(2,1)} async-done(((bf16[640,640]{0,1:T(8,128)(2,1)}), bf16[2560,640]{0,1:T(8,128)(2,1)}) %all-gather.26.cloned.1.call-update) | async-done | bytes 3276816 | tf_op jit(solution)/shard_map/all_gather | solution.py:112
  409.0 51.8 %while.53 = (s32[]{:T(128)}, bf16[5,640,64]{1,2,0:T(8,128)(2,1)}, f32[5,640]{1,0:T(8,128)S(1)}, bf16[5,640,64]{2,1,0:T(8,128)(2,1)}, bf16[5,2560,64]{2,1,0:T(8,1...) while((s32[]{:T(128)}, bf16[5,640,64]{1,2,0:T(8,128)(2,1)}, ...), condition=%wide.region_17.18_spmd, body=%wide.region_14.17_spmd.sunk | while | flops 432536960 | bytes 49184892 | solution.py:132
  414.4 5.2 fusion.309
  425.0 5.0 fusion.309
  435.3 5.0 fusion.309
  445.6 4.9 fusion.309
  455.9 4.9 fusion.309
  465.3 8.9 multiply_reduce_fusion.3
  483.8 17.6 %reduce-scatter.26.cloned.1.call-done = bf16[160,1280]{1,0:T(8,128)(2,1)} async-done(((bf16[640,1280]{1,0:T(8,128)(2,1)}), bf16[160,1280]{1,0:T(8,128)(2,1)}) %reduce-scatter.26.cloned.1.call-update) | async-done | bytes 409616 | tf_op jit(solution)/shard_map/reduce_scatter | solution.py:71
  502.6 36.5 %reduce-scatter.30.cloned.1.call-done = bf16[160,1280]{1,0:T(8,128)(2,1)} async-done(((bf16[640,1280]{1,0:T(8,128)(2,1)}), bf16[160,1280]{1,0:T(8,128)(2,1)}) %reduce-scatter.30.cloned.1.call-update) | async-done | bytes 409616 | tf_op jit(solution)/shard_map/reduce_scatter | solution.py:71
  543.0 37.1 %all-gather.28.cloned.1.call-done = bf16[640,1280]{1,0:T(8,128)(2,1)} async-done(((bf16[160,1280]{1,0:T(8,128)(2,1)}), bf16[640,1280]{1,0:T(8,128)(2,1)}) %all-gather.28.cloned.1.call-update) | async-done | bytes 1638416 | tf_op jit(solution)/shard_map/all_gather | solution.py:59
  594.0 35.3 %reduce-scatter.28.cloned.1.call-done = bf16[160,1280]{1,0:T(8,128)(2,1)} async-done(((bf16[640,1280]{1,0:T(8,128)(2,1)}), bf16[160,1280]{1,0:T(8,128)(2,1)}) %reduce-scatter.28.cloned.1.call-update) | async-done | bytes 409616 | tf_op jit(solution)/shard_map/reduce_scatter | solution.py:71
  636.0 36.7 %all-gather.34.cloned.1.call-done = bf16[640,1280]{1,0:T(8,128)(2,1)} async-done(((bf16[160,1280]{1,0:T(8,128)(2,1)}), bf16[640,1280]{1,0:T(8,128)(2,1)}) %all-gather.34.cloned.1.call-update) | async-done | bytes 1638416 | tf_op jit(solution)/shard_map/all_gather | solution.py:63
  672.7 8.8 multiply_reduce_fusion.2
  690.5 35.2 %reduce-scatter.34.cloned.1.call-done = bf16[160,1280]{1,0:T(8,128)(2,1)} async-done(((bf16[640,1280]{1,0:T(8,128)(2,1)}), bf16[160,1280]{1,0:T(8,128)(2,1)}) %reduce-scatter.34.cloned.1.call-update) | async-done | bytes 409616 | tf_op jit(solution)/shard_map/reduce_scatter | solution.py:71
  734.0 34.7 %all-gather.32.cloned.1.call-done = bf16[640,1280]{1,0:T(8,128)(2,1)} async-done(((bf16[160,1280]{1,0:T(8,128)(2,1)}), bf16[640,1280]{1,0:T(8,128)(2,1)}) %all-gather.32.cloned.1.call-update) | async-done | bytes 1638416 | tf_op jit(solution)/shard_map/all_gather | solution.py:63
  775.3 71.4 %while.54 = (s32[]{:T(128)}, f32[5,640,64]{1,2,0:T(8,128)S(1)}, bf16[5,2560,64]{1,2,0:T(8,128)(2,1)}, bf16[5,2560,64]{1,2,0:T(8,128)(2,1)}, bf16[5,640,64]{2,1,0...) while((s32[]{:T(128)}, f32[5,640,64]{1,2,0:T(8,128)S(1)}, ...), condition=%wide.region_31.32_spmd, body=%wide.region_29.31_spmd.sunk | while | flops 1063525760 | bytes 61458068 | solution.py:208
  860.6 71.4 %while.55 = (s32[]{:T(128)}, f32[5,640,64]{1,2,0:T(8,128)S(1)}, bf16[5,2560,64]{1,2,0:T(8,128)(2,1)}, bf16[5,2560,64]{1,2,0:T(8,128)(2,1)}, bf16[5,640,64]{2,1,0...) while((s32[]{:T(128)}, f32[5,640,64]{1,2,0:T(8,128)S(1)}, ...), condition=%wide.region_43.44_spmd, body=%wide.region_41.43_spmd.sunk | while | flops 1063525760 | bytes 61458068 | solution.py:208
  940.4 7.9 convolution_convert_fusion
  953.0 6.0 convolution_convert_fusion.1
  960.9 7.9 convolution_convert_fusion.2
  968.9 5.2 fusion.104
  985.2 5.1 convolution_convert_fusion.9
  1002.4 5.0 convolution_convert_fusion.10
  1020.0 6.6 reduce-scatter.50.cloned.1.call-done
  1028.6 48.3 %reduce-scatter.48.cloned.1.call-done = bf16[160,1280]{1,0:T(8,128)(2,1)} async-done(((bf16[1280,1280]{1,0:T(8,128)(2,1)}), bf16[160,1280]{1,0:T(8,128)(2,1)}) %reduce-scatter.48.cloned.1.call-update) | async-done | bytes 409616 | tf_op jit(solution)/shard_map/reduce_scatter | solution.py:290
  1078.8 48.2 %reduce-scatter.46.cloned.1.call-done = bf16[160,1280]{1,0:T(8,128)(2,1)} async-done(((bf16[1280,1280]{1,0:T(8,128)(2,1)}), bf16[160,1280]{1,0:T(8,128)(2,1)}) %reduce-scatter.46.cloned.1.call-update) | async-done | bytes 409616 | tf_op jit(solution)/shard_map/reduce_scatter | solution.py:290
  1129.1 36.7 %reduce-scatter.44.cloned.1.call-done = bf16[320,160]{0,1:T(8,128)(2,1)} async-done(((bf16[320,1280]{0,1:T(8,128)(2,1)}), bf16[320,160]{0,1:T(8,128)(2,1)}) %reduce-scatter.44.cloned.1.call-update) | async-done | bytes 102416 | tf_op jit(solution)/shard_map/reduce_scatter | solution.py:290
  1167.5 37.6 %reduce-scatter.38.cloned.1.call-done = bf16[160,320]{1,0:T(8,128)(2,1)} async-done(((bf16[1280,320]{1,0:T(8,128)(2,1)}), bf16[160,320]{1,0:T(8,128)(2,1)}) %reduce-scatter.38.cloned.1.call-update) | async-done | bytes 102416 | tf_op jit(solution)/shard_map/reduce_scatter | solution.py:290
  1206.7 40.9 %all-reduce = (f32[1280]{0:T(1024)}, f32[1280]{0:T(1024)}, f32[1280]{0:T(1024)S(1)}, f32[5120]{0:T(1024)S(1)}, f32[5120]{0:T(1024)S(1)}) all-reduce(f32[1280]{0:T(1024)S(1)} %add.328, f32[1280]{0:T(1024)S(1)} %add.329, f32[1280]{0:T(1024)S(1)} %add_dynamic-update-slice_fusion.1, ...), channel_id=1, replica_groups=mesh['shard'=2,'ctx'=4,'tp'=4] {'shard','ctx','tp'}, use_global_device_ids=true, to_apply=%region_57.58 | all-reduce | flops 14080 | bytes 112640 | tf_op jit(solution)/shard_map/psum | solution.py:316
  1251.3 32.1 %reduce-scatter.40.cloned.1.call-done = bf16[160,320]{1,0:T(8,128)(2,1)} async-done(((bf16[1280,320]{1,0:T(8,128)(2,1)}), bf16[160,320]{1,0:T(8,128)(2,1)}) %reduce-scatter.40.cloned.1.call-update) | async-done | bytes 102416 | tf_op jit(solution)/shard_map/reduce_scatter | solution.py:290
  1285.0 36.9 %reduce-scatter.36.cloned.1.call-done = bf16[160,1280]{1,0:T(8,128)(2,1)} async-done(((bf16[640,1280]{1,0:T(8,128)(2,1)}), bf16[160,1280]{1,0:T(8,128)(2,1)}) %reduce-scatter.36.cloned.1.call-update) | async-done | bytes 409616 | tf_op jit(solution)/shard_map/reduce_scatter | solution.py:71
  1321.9 38.3 %reduce-scatter.32.cloned.1.call-done = bf16[160,1280]{1,0:T(8,128)(2,1)} async-done(((bf16[640,1280]{1,0:T(8,128)(2,1)}), bf16[160,1280]{1,0:T(8,128)(2,1)}) %reduce-scatter.32.cloned.1.call-update) | async-done | bytes 409616 | tf_op jit(solution)/shard_map/reduce_scatter | solution.py:71
  (632 shorter events, 455.7 us)
Async XLA Ops:
  8.0 43.9 %all-gather.40.cloned.1.call-start = ((), (), s32[]{:S(2)}) async-start(), calls=%async_computation.44 | async-start | bytes 2048000 | tf_op jit(solution)/shard_map/all_gather | solution.py:59
  10.2 80.9 %all-gather.38.cloned.1.call-start = ((), (), s32[]{:S(2)}) async-start(), calls=%async_computation.43 | async-start | bytes 2048000 | tf_op jit(solution)/shard_map/all_gather | solution.py:59
  11.0 128.2 %all-gather.16.cloned.1.call-start = ((), (), s32[]{:S(2)}) async-start(), calls=%async_computation.17 | async-start | bytes 4096000 | tf_op jit(solution)/shard_map/all_gather | solution.py:112
  35.4 62.4 %copy-start.9 = (bf16[1280,320]{1,0:T(8,128)(2,1)}, bf16[1280,320]{1,0:T(8,128)(2,1)S(1)}, u32[]{:S(2)}) copy-start(bf16[1280,320]{1,0:T(8,128)(2,1)S(1)} %all_gather.53) | copy-start | bytes 2457604
  54.5 48.1 %copy-start.15 = (f32[640,320]{0,1:T(8,128)}, f32[640,320]{0,1:T(8,128)S(1)}, u32[]{:S(2)}) copy-start(f32[640,320]{0,1:T(8,128)S(1)} %fusion.165) | copy-start | bytes 2457604
  54.6 39.2 %copy-start.83 = (f32[640,5]{0,1:T(8,128)}, f32[640,5]{0,1:T(8,128)S(1)}, u32[]{:S(2)}) copy-start(f32[640,5]{0,1:T(8,128)S(1)} %multiply_reduce_fusion.18) | copy-start | bytes 38404
  54.6 48.0 %copy-start.73 = (f32[640,5]{0,1:T(8,128)}, f32[640,5]{0,1:T(8,128)S(1)}, u32[]{:S(2)}) copy-start(f32[640,5]{0,1:T(8,128)S(1)} %add_rsqrt_fusion.1) | copy-start | bytes 38404
  108.4 138.4 %reduce-scatter.22.cloned.1.call-start = ((), (), s32[]{:S(2)}) async-start(), calls=%async_computation.18 | async-start | bytes 2048000 | tf_op jit(solution)/shard_map/reduce_scatter | solution.py:71
  150.4 57.9 %copy-start.66 = (bf16[320,1280]{0,1:T(8,128)(2,1)S(1)}, bf16[320,1280]{0,1:T(8,128)(2,1)}, u32[]{:S(2)}) copy-start(bf16[320,1280]{0,1:T(8,128)(2,1)} %all_gather.56) | copy-start | bytes 2457604
  208.3 44.3 %copy-start.2 = (pred[640,2560]{1,0:T(32,128)(4,1)}, pred[640,2560]{1,0:T(32,128)(4,1)S(1)}, u32[]{:S(2)}) copy-start(pred[640,2560]{1,0:T(32,128)(4,1)S(1)} %get-tuple-element.781) | copy-start | bytes 4915204
  208.3 40.2 %copy-start.8 = (bf16[2,1,160,1280]{3,2,1,0:T(8,128)(2,1)S(1)}, bf16[2,1,160,1280]{3,2,1,0:T(8,128)(2,1)}, u32[]{:S(2)}) copy-start(bf16[2,1,160,1280]{3,2,1,0:T(8,128)(2,1)} %param.24) | copy-start | bytes 2457604
  208.3 40.2 %copy-start.68 = (f32[1280]{0:T(1024)S(1)}, f32[1280]{0:T(1024)}, u32[]{:S(2)}) copy-start(f32[1280]{0:T(1024)} %param.34) | copy-start | bytes 15364
  211.9 42.1 %copy-start.29 = (bf16[1280,320]{1,0:T(8,128)(2,1)S(1)}, bf16[1280,320]{1,0:T(8,128)(2,1)}, u32[]{:S(2)}) copy-start(bf16[1280,320]{1,0:T(8,128)(2,1)} %all_gather.54) | copy-start | bytes 2457604
  211.9 45.5 %all-gather.22.cloned.1.call-start = ((), (), s32[]{:S(2)}) async-start(), calls=%async_computation.21 | async-start | bytes 3686400 | tf_op jit(solution)/shard_map/all_gather | solution.py:263
  212.5 77.3 %all-gather.18.cloned.1.call-start = ((), (), s32[]{:S(2)}) async-start(), calls=%async_computation.19 | async-start | bytes 2048000 | tf_op jit(solution)/shard_map/all_gather | solution.py:59
  252.7 70.6 %all-gather.20.cloned.1.call-start = ((), (), s32[]{:S(2)}) async-start(), calls=%async_computation.20 | async-start | bytes 3686400 | tf_op jit(solution)/shard_map/all_gather | solution.py:262
  253.2 104.8 %all-gather.24.cloned.1.call-start = ((), (), s32[]{:S(2)}) async-start(), calls=%async_computation.22 | async-start | bytes 3686400 | tf_op jit(solution)/shard_map/all_gather | solution.py:264
  254.0 134.9 %all-gather.26.cloned.1.call-start = ((), (), s32[]{:S(2)}) async-start(), calls=%async_computation.24 | async-start | bytes 4096000 | tf_op jit(solution)/shard_map/all_gather | solution.py:112
  257.3 144.4 %reduce-scatter.24.cloned.1.call-start = ((), (), s32[]{:S(2)}) async-start(), calls=%async_computation.23 | async-start | bytes 2048000 | tf_op jit(solution)/shard_map/reduce_scatter | solution.py:71
  257.4 65.9 %copy-start.118 = (f32[1280]{0:T(1024)S(1)}, f32[1280]{0:T(1024)}, u32[]{:S(2)}) copy-start(f32[1280]{0:T(1024)} %param.37) | copy-start | bytes 15364
  364.0 101.3 %all-gather.30.cloned.1.call-start = ((), (), s32[]{:S(2)}) async-start(), calls=%async_computation.28 | async-start | bytes 2048000 | tf_op jit(solution)/shard_map/all_gather | solution.py:63
  409.0 92.4 %reduce-scatter.26.cloned.1.call-start = ((), (), s32[]{:S(2)}) async-start(), calls=%async_computation.25 | async-start | bytes 2048000 | tf_op jit(solution)/shard_map/reduce_scatter | solution.py:71
  465.0 74.1 %reduce-scatter.30.cloned.1.call-start = ((), (), s32[]{:S(2)}) async-start(), calls=%async_computation.29 | async-start | bytes 2048000 | tf_op jit(solution)/shard_map/reduce_scatter | solution.py:71
  480.3 58.9 %copy-start.23 = (f32[160,1280]{1,0:T(8,128)S(1)}, f32[160,1280]{1,0:T(8,128)}, u32[]{:S(2)}) copy-start(f32[160,1280]{1,0:T(8,128)} %copy-done.22) | copy-start | bytes 2457604
  483.8 96.4 %all-gather.28.cloned.1.call-start = ((), (), s32[]{:S(2)}) async-start(), calls=%async_computation.26 | async-start | bytes 2048000 | tf_op jit(solution)/shard_map/all_gather | solution.py:59
  501.4 40.4 %copy-start.12 = (bf16[160,1280]{1,0:T(8,128)(2,1)S(1)}, bf16[160,1280]{1,0:T(8,128)(2,1)}, u32[]{:S(2)}) copy-start(bf16[160,1280]{1,0:T(8,128)(2,1)} %reduce-scatter.26.cloned.1.call-done) | copy-start | bytes 1228804
  543.0 86.3 %reduce-scatter.28.cloned.1.call-start = ((), (), s32[]{:S(2)}) async-start(), calls=%async_computation.27 | async-start | bytes 2048000 | tf_op jit(solution)/shard_map/reduce_scatter | solution.py:71
  590.4 40.1 %copy-start.37 = (bf16[2,1,160,1280]{3,2,1,0:T(8,128)(2,1)S(1)}, bf16[2,1,160,1280]{3,2,1,0:T(8,128)(2,1)}, u32[]{:S(2)}) copy-start(bf16[2,1,160,1280]{3,2,1,0:T(8,128)(2,1)} %param.39) | copy-start | bytes 2457604
  594.0 78.7 %all-gather.34.cloned.1.call-start = ((), (), s32[]{:S(2)}) async-start(), calls=%async_computation.32 | async-start | bytes 2048000 | tf_op jit(solution)/shard_map/all_gather | solution.py:63
  635.5 90.2 %reduce-scatter.34.cloned.1.call-start = ((), (), s32[]{:S(2)}) async-start(), calls=%async_computation.33 | async-start | bytes 2048000 | tf_op jit(solution)/shard_map/reduce_scatter | solution.py:71
  686.9 38.9 %copy-start.62 = (bf16[160,1280]{1,0:T(8,128)(2,1)S(1)}, bf16[160,1280]{1,0:T(8,128)(2,1)}, u32[]{:S(2)}) copy-start(bf16[160,1280]{1,0:T(8,128)(2,1)} %reduce-scatter.30.cloned.1.call-done) | copy-start | bytes 1228804
  690.5 78.2 %all-gather.32.cloned.1.call-start = ((), (), s32[]{:S(2)}) async-start(), calls=%async_computation.30 | async-start | bytes 2048000 | tf_op jit(solution)/shard_map/all_gather | solution.py:63
  731.5 121.9 %all-gather.36.cloned.1.call-start = ((), (), s32[]{:S(2)}) async-start(), calls=%async_computation.34 | async-start | bytes 2048000 | tf_op jit(solution)/shard_map/all_gather | solution.py:63
  733.7 245.9 %reduce-scatter.52.cloned.1.call-start = ((), (), s32[]{:S(2)}) async-start(), calls=%async_computation.45 | async-start | bytes 4096000
  853.2 128.9 %reduce-scatter.54.cloned.1.call-start = ((), (), s32[]{:S(2)}) async-start(), calls=%async_computation.46 | async-start | bytes 4096000
  938.5 88.2 %reduce-scatter.50.cloned.1.call-start = ((), (), s32[]{:S(2)}) async-start(), calls=%async_computation.42 | async-start | bytes 3686400 | tf_op jit(solution)/shard_map/reduce_scatter | solution.py:290
  948.3 128.6 %reduce-scatter.48.cloned.1.call-start = ((), (), s32[]{:S(2)}) async-start(), calls=%async_computation.41 | async-start | bytes 3686400 | tf_op jit(solution)/shard_map/reduce_scatter | solution.py:290
  959.0 168.0 %reduce-scatter.46.cloned.1.call-start = ((), (), s32[]{:S(2)}) async-start(), calls=%async_computation.40 | async-start | bytes 3686400 | tf_op jit(solution)/shard_map/reduce_scatter | solution.py:290
  968.8 197.0 %reduce-scatter.44.cloned.1.call-start = ((), (), s32[]{:S(2)}) async-start(), calls=%async_computation.39 | async-start | bytes 1105920 | tf_op jit(solution)/shard_map/reduce_scatter | solution.py:290
  974.1 230.9 %reduce-scatter.38.cloned.1.call-start = ((), (), s32[]{:S(2)}) async-start(), calls=%async_computation.36 | async-start | bytes 1105920 | tf_op jit(solution)/shard_map/reduce_scatter | solution.py:290
  979.1 270.6 %reduce-scatter.42.cloned.1.call-start = ((), (), s32[]{:S(2)}) async-start(), calls=%async_computation.38 | async-start | bytes 1105920 | tf_op jit(solution)/shard_map/reduce_scatter | solution.py:290
  990.3 293.1 %reduce-scatter.40.cloned.1.call-start = ((), (), s32[]{:S(2)}) async-start(), calls=%async_computation.37 | async-start | bytes 1105920 | tf_op jit(solution)/shard_map/reduce_scatter | solution.py:290
  1007.4 314.5 %reduce-scatter.36.cloned.1.call-start = ((), (), s32[]{:S(2)}) async-start(), calls=%async_computation.35 | async-start | bytes 2048000 | tf_op jit(solution)/shard_map/reduce_scatter | solution.py:71
  1012.5 347.7 %reduce-scatter.32.cloned.1.call-start = ((), (), s32[]{:S(2)}) async-start(), calls=%async_computation.31 | async-start | bytes 2048000 | tf_op jit(solution)/shard_map/reduce_scatter | solution.py:71
  1018.6 110.4 %copy-start.36 = (f32[640,320]{0,1:T(8,128)S(1)}, f32[640,320]{0,1:T(8,128)}, u32[]{:S(2)}) copy-start(f32[640,320]{0,1:T(8,128)} %get-tuple-element.387) | copy-start | bytes 2457604
  1019.9 340.3 %copy-start.32 = (f32[160,1280]{1,0:T(8,128)S(1)}, f32[160,1280]{1,0:T(8,128)}, u32[]{:S(2)}) copy-start(f32[160,1280]{1,0:T(8,128)} %get-tuple-element.332) | copy-start | bytes 2457604
  1020.0 340.3 %copy-start.34 = (f32[160,1280]{1,0:T(8,128)S(1)}, f32[160,1280]{1,0:T(8,128)}, u32[]{:S(2)}) copy-start(f32[160,1280]{1,0:T(8,128)} %copy-done.33) | copy-start | bytes 2457604
  1020.0 340.3 %copy-start.69 = (f32[1280]{0:T(1024)S(1)}, f32[1280]{0:T(1024)}, u32[]{:S(2)}) copy-start(f32[1280]{0:T(1024)} %param.34) | copy-start | bytes 15364
  (121 other events, 541.9 us)
Sparse Core Ops, SparseCore 0:
  11.0 40.8 all-gather.39
  54.0 37.0 all-gather.37
  108.5 30.6 all-gather.15
  212.1 34.6 reduce-scatter.21
  364.1 36.2 reduce-scatter.23
  409.1 38.1 all-gather.29
  465.2 36.1 reduce-scatter.25
  503.8 35.3 reduce-scatter.29
  594.1 35.1 reduce-scatter.27
  690.6 35.1 reduce-scatter.33
  853.3 37.6 reduce-scatter.51
  938.6 37.6 reduce-scatter.53
  979.7 46.8 reduce-scatter.49
  1029.9 46.9 reduce-scatter.47
  1080.1 46.8 reduce-scatter.45
  1130.1 35.7 reduce-scatter.43
  1169.2 35.7 reduce-scatter.37
  1208.1 35.8 reduce-scatter.41
  1247.5 35.8 reduce-scatter.39
  1285.5 36.3 reduce-scatter.35
  1324.9 35.2 reduce-scatter.31
Sparse Core Ops, SparseCore 1:
  214.4 31.0 all-gather.21
  252.7 37.0 all-gather.17
  291.7 31.5 all-gather.19
  325.3 32.7 all-gather.23
  359.6 29.1 all-gather.25
  543.1 37.0 all-gather.27
  635.6 37.0 all-gather.33
  731.6 37.0 all-gather.31
  770.2 36.8 all-gather.35
where the time goes:
time: 1380 us; the launch traced here: 1370 us
  waiting for transfers between devices  707 us (51%)
  matrix products  354 us (26%)
  local copies, waits for them, and re-layouts  111 us (8%)
  blocking collectives  92.6 us (7%)
  other arithmetic  84.3 us (6%)
  between operations  17.7 us (1%)
    reduce_scatter x8, waiting for transfers between devices, own_grads(): lax.psum_scatter(partial_value.astype(jnp.bfloat16), 'tp', scatter_dimens...  234 us
    reduce_scatter x7, waiting for transfers between devices, to_owner(): lax.psum_scatter(product, spread, scatter_dimension=axis, tiled=True)  210 us
    dot_general x44, matrix products, contract_cols(): lax.dot_general(former, latter, (((1,), (1,)), ((), ())), preferred_eleme...  127 us
    all_gather x4, waiting for transfers between devices, group_rows(): return lax.all_gather(own_block, 'tp', axis=0, tiled=True)  110 us
    dot_general x27, matrix products, contract_rows(): lax.dot_general(former, latter, (((0,), (0,)), ((), ())), preferred_eleme...  88.9 us
    all_gather x4, waiting for transfers between devices, group_grads(): return lax.all_gather(own_block, 'tp', axis=0, tiled=True)  71.4 us
    dot_general x10, matrix products, head_forward(): jnp.dot(soft_weights.astype(jnp.bfloat16), value_one, preferred_element_t...  49.6 us
    psum x1, blocking collectives, per_device(): lax.psum((sum_attn, sum_mlp, padded(sum_qk), padded(sum_up), padded(sum_g...  40.9 us
  transfers between devices with their start and end apart: 30, of which 23 were waited for; matrix products, arithmetic and copies ran while one was open for 27% of the time, Pallas kernels for 0%

commit v1 on v0

--- a/solution.py
+++ b/solution.py
@@ -314,8 +314,10 @@
         )
 
     alpha_attn_sum, alpha_mlp_sum, qk_sum, up_sum, gate_sum = lax.psum(
-        (sum_attn, sum_mlp, padded(sum_qk), padded(sum_up), padded(sum_gate)),
-        ("shard", "ctx", "tp"),
+        lax.psum(
+            (sum_attn, sum_mlp, padded(sum_qk), padded(sum_up), padded(sum_gate)), ("ctx", "tp")
+        ),
+        "shard",
     )
     return (
         jnp.stack([mid[m][0] for m in micros])[:, None],

time: 1380 us -> 1380 us (level)
  blocking collectives: 92.6 us -> 122 us
  waiting for transfers between devices: 707 us -> 678 us
    reduce_scatter x7, waiting for transfers between devices: 210 us -> 180 us  [to_owner(): lax.psum_scatter(product, spread, scatter_dimension=axis, tiled=True)]
    psum x1, blocking collectives: 40.9 us -> 61.5 us  [per_device(): lax.psum((sum_attn, sum_mlp, padded(sum_qk), padded(sum_up), padded(sum_g...]
where the time goes in v1:
time: 1380 us; the launch traced here: 1370 us
  waiting for transfers between devices  678 us (49%)
  matrix products  354 us (26%)
  blocking collectives  122 us (9%)
  local copies, waits for them, and re-layouts  111 us (8%)
  other arithmetic  84.3 us (6%)
  between operations  17.7 us (1%)
    reduce_scatter x8, waiting for transfers between devices, own_grads(): lax.psum_scatter(partial_value.astype(jnp.bfloat16), 'tp', scatter_dimens...  234 us
    reduce_scatter x7, waiting for transfers between devices, to_owner(): lax.psum_scatter(product, spread, scatter_dimension=axis, tiled=True)  180 us
    dot_general x44, matrix products, contract_cols(): lax.dot_general(former, latter, (((1,), (1,)), ((), ())), preferred_eleme...  127 us
    all_gather x4, waiting for transfers between devices, group_rows(): return lax.all_gather(own_block, 'tp', axis=0, tiled=True)  110 us
    dot_general x27, matrix products, contract_rows(): lax.dot_general(former, latter, (((0,), (0,)), ((), ())), preferred_eleme...  88.9 us
    all_gather x4, waiting for transfers between devices, group_grads(): return lax.all_gather(own_block, 'tp', axis=0, tiled=True)  71.4 us
    psum x1, blocking collectives, per_device(): lax.psum((sum_attn, sum_mlp, padded(sum_qk), padded(sum_up), padded(sum_g...  61.5 us
    dot_general x10, matrix products, head_forward(): jnp.dot(soft_weights.astype(jnp.bfloat16), value_one, preferred_element_t...  49.6 us
  transfers between devices with their start and end apart: 30, of which 23 were waited for; matrix products, arithmetic and copies ran while one was open for 27% of the time, Pallas kernels for 0%

profile of v1, /device:TPU:0, one launch (start us, length us, event | category | flops | bytes accessed | tf_op | source)
XLA Modules:
  0.0 1370.8 jit_solution(6894940005163655728)
XLA Ops:
  11.0 14.3 %all_gather.52 = bf16[1280,320]{1,0:T(8,128)(2,1)} all-gather(bf16[160,320]{1,0:T(8,128)(2,1)} %param.27), channel_id=1, replica_groups=mesh['shard'=2,'ctx'=4,'tp'=4] {'shard','ctx'}, dimensions={0}, use_global_device_ids=true | all-gather | bytes 921600 | tf_op jit(solution)/shard_map/all_gather | solution.py:258
  25.3 10.2 all_gather.53
  35.4 12.0 all_gather.54
  54.6 36.5 %all-gather.38.cloned.1.call-done = bf16[1,1,640,1280]{3,2,1,0:T(8,128)(2,1)} async-done(((bf16[1,1,160,1280]{3,2,1,0:T(8,128)(2,1)}), bf16[1,1,640,1280]{3,2,1,0:T(8,128)(2,1)}) %all-gather.38.cloned.1.call-update) | async-done | bytes 1638416 | tf_op jit(solution)/shard_map/all_gather | solution.py:59
  109.7 15.3 %all_gather.56 = bf16[320,1280]{0,1:T(8,128)(2,1)} all-gather(bf16[320,160]{0,1:T(8,128)(2,1)S(1)} %copy-done.91), channel_id=1, replica_groups=mesh['shard'=2,'ctx'=4,'tp'=4] {'shard','ctx'}, dimensions={1}, use_global_device_ids=true | all-gather | bytes 921600 | tf_op jit(solution)/shard_map/all_gather | solution.py:261
  131.8 7.4 all-gather.16.cloned.1.call-done
  150.4 57.9 %while.52 = (s32[]{:T(128)}, bf16[5,640,64]{1,2,0:T(8,128)(2,1)}, f32[5,640]{1,0:T(8,128)}, bf16[5,640,64]{2,1,0:T(8,128)(2,1)}, bf16[5,2560,64]{2,1,0:T(8,128)(...) while((s32[]{:T(128)}, bf16[5,640,64]{1,2,0:T(8,128)(2,1)}, ...), condition=%wide.region_5.6_spmd, body=%wide.region_2.5_spmd.sunk | while | flops 432536960 | bytes 49184892 | solution.py:132
  157.1 4.9 fusion.305
  168.7 4.9 fusion.305
  213.1 33.7 %reduce-scatter.22.cloned.1.call-done = bf16[160,1280]{1,0:T(8,128)(2,1)} async-done(((bf16[640,1280]{1,0:T(8,128)(2,1)}), bf16[160,1280]{1,0:T(8,128)(2,1)}) %reduce-scatter.22.cloned.1.call-update) | async-done | bytes 409616 | tf_op jit(solution)/shard_map/reduce_scatter | solution.py:71
  257.5 32.4 %all-gather.18.cloned.1.call-done = bf16[640,1280]{1,0:T(8,128)(2,1)} async-done(((bf16[160,1280]{1,0:T(8,128)(2,1)}), bf16[640,1280]{1,0:T(8,128)(2,1)}) %all-gather.18.cloned.1.call-update) | async-done | bytes 1638416 | tf_op jit(solution)/shard_map/all_gather | solution.py:59
  289.8 6.5 fusion.186
  296.3 27.0 %all-gather.20.cloned.1.call-done = bf16[1280,1280]{1,0:T(8,128)(2,1)} async-done(((bf16[160,1280]{1,0:T(8,128)(2,1)}), bf16[1280,1280]{1,0:T(8,128)(2,1)}) %all-gather.20.cloned.1.call-update) | async-done | bytes 3276816 | tf_op jit(solution)/shard_map/all_gather | solution.py:262
  323.3 7.6 multiply_convert_fusion.7
  330.9 27.2 %all-gather.24.cloned.1.call-done = bf16[1280,1280]{0,1:T(8,128)(2,1)} async-done(((bf16[1280,160]{0,1:T(8,128)(2,1)}), bf16[1280,1280]{0,1:T(8,128)(2,1)}) %all-gather.24.cloned.1.call-update) | async-done | bytes 3276816 | tf_op jit(solution)/shard_map/all_gather | solution.py:264
  358.1 5.9 convolution_convert_fusion.7
  371.2 17.7 %all-gather.26.cloned.1.call-done = bf16[2560,640]{0,1:T(8,128)(2,1)} async-done(((bf16[640,640]{0,1:T(8,128)(2,1)}), bf16[2560,640]{0,1:T(8,128)(2,1)}) %all-gather.26.cloned.1.call-update) | async-done | bytes 3276816 | tf_op jit(solution)/shard_map/all_gather | solution.py:112
  409.1 51.7 %while.53 = (s32[]{:T(128)}, bf16[5,640,64]{1,2,0:T(8,128)(2,1)}, f32[5,640]{1,0:T(8,128)S(1)}, bf16[5,640,64]{2,1,0:T(8,128)(2,1)}, bf16[5,2560,64]{2,1,0:T(8,1...) while((s32[]{:T(128)}, bf16[5,640,64]{1,2,0:T(8,128)(2,1)}, ...), condition=%wide.region_17.18_spmd, body=%wide.region_14.17_spmd.sunk | while | flops 432536960 | bytes 49184892 | solution.py:132
  414.4 5.2 fusion.309
  425.0 5.0 fusion.309
  435.3 5.0 fusion.309
  445.6 4.9 fusion.309
  465.3 8.9 multiply_reduce_fusion.3
  483.8 17.6 %reduce-scatter.26.cloned.1.call-done = bf16[160,1280]{1,0:T(8,128)(2,1)} async-done(((bf16[640,1280]{1,0:T(8,128)(2,1)}), bf16[160,1280]{1,0:T(8,128)(2,1)}) %reduce-scatter.26.cloned.1.call-update) | async-done | bytes 409616 | tf_op jit(solution)/shard_map/reduce_scatter | solution.py:71
  502.6 36.5 %reduce-scatter.30.cloned.1.call-done = bf16[160,1280]{1,0:T(8,128)(2,1)} async-done(((bf16[640,1280]{1,0:T(8,128)(2,1)}), bf16[160,1280]{1,0:T(8,128)(2,1)}) %reduce-scatter.30.cloned.1.call-update) | async-done | bytes 409616 | tf_op jit(solution)/shard_map/reduce_scatter | solution.py:71
  543.0 37.1 %all-gather.28.cloned.1.call-done = bf16[640,1280]{1,0:T(8,128)(2,1)} async-done(((bf16[160,1280]{1,0:T(8,128)(2,1)}), bf16[640,1280]{1,0:T(8,128)(2,1)}) %all-gather.28.cloned.1.call-update) | async-done | bytes 1638416 | tf_op jit(solution)/shard_map/all_gather | solution.py:59
  594.0 35.3 %reduce-scatter.28.cloned.1.call-done = bf16[160,1280]{1,0:T(8,128)(2,1)} async-done(((bf16[640,1280]{1,0:T(8,128)(2,1)}), bf16[160,1280]{1,0:T(8,128)(2,1)}) %reduce-scatter.28.cloned.1.call-update) | async-done | bytes 409616 | tf_op jit(solution)/shard_map/reduce_scatter | solution.py:71
  636.0 36.7 %all-gather.34.cloned.1.call-done = bf16[640,1280]{1,0:T(8,128)(2,1)} async-done(((bf16[160,1280]{1,0:T(8,128)(2,1)}), bf16[640,1280]{1,0:T(8,128)(2,1)}) %all-gather.34.cloned.1.call-update) | async-done | bytes 1638416 | tf_op jit(solution)/shard_map/all_gather | solution.py:63
  672.6 8.8 multiply_reduce_fusion.2
  690.5 35.2 %reduce-scatter.34.cloned.1.call-done = bf16[160,1280]{1,0:T(8,128)(2,1)} async-done(((bf16[640,1280]{1,0:T(8,128)(2,1)}), bf16[160,1280]{1,0:T(8,128)(2,1)}) %reduce-scatter.34.cloned.1.call-update) | async-done | bytes 409616 | tf_op jit(solution)/shard_map/reduce_scatter | solution.py:71
  733.9 34.7 %all-gather.32.cloned.1.call-done = bf16[640,1280]{1,0:T(8,128)(2,1)} async-done(((bf16[160,1280]{1,0:T(8,128)(2,1)}), bf16[640,1280]{1,0:T(8,128)(2,1)}) %all-gather.32.cloned.1.call-update) | async-done | bytes 1638416 | tf_op jit(solution)/shard_map/all_gather | solution.py:63
  775.2 71.4 %while.54 = (s32[]{:T(128)}, f32[5,640,64]{1,2,0:T(8,128)S(1)}, bf16[5,2560,64]{1,2,0:T(8,128)(2,1)}, bf16[5,2560,64]{1,2,0:T(8,128)(2,1)}, bf16[5,640,64]{2,1,0...) while((s32[]{:T(128)}, f32[5,640,64]{1,2,0:T(8,128)S(1)}, ...), condition=%wide.region_31.32_spmd, body=%wide.region_29.31_spmd.sunk | while | flops 1063525760 | bytes 61458068 | solution.py:208
  860.5 71.4 %while.55 = (s32[]{:T(128)}, f32[5,640,64]{1,2,0:T(8,128)S(1)}, bf16[5,2560,64]{1,2,0:T(8,128)(2,1)}, bf16[5,2560,64]{1,2,0:T(8,128)(2,1)}, bf16[5,640,64]{2,1,0...) while((s32[]{:T(128)}, f32[5,640,64]{1,2,0:T(8,128)S(1)}, ...), condition=%wide.region_43.44_spmd, body=%wide.region_41.43_spmd.sunk | while | flops 1063525760 | bytes 61458068 | solution.py:208
  940.3 7.9 convolution_convert_fusion
  952.9 6.0 convolution_convert_fusion.1
  960.8 7.9 convolution_convert_fusion.2
  968.8 5.2 fusion.104
  985.1 5.1 convolution_convert_fusion.9
  1002.3 5.0 convolution_convert_fusion.10
  1019.9 6.7 reduce-scatter.50.cloned.1.call-done
  1028.5 48.2 %reduce-scatter.48.cloned.1.call-done = bf16[160,1280]{1,0:T(8,128)(2,1)} async-done(((bf16[1280,1280]{1,0:T(8,128)(2,1)}), bf16[160,1280]{1,0:T(8,128)(2,1)}) %reduce-scatter.48.cloned.1.call-update) | async-done | bytes 409616 | tf_op jit(solution)/shard_map/reduce_scatter | solution.py:290
  1078.7 48.2 %reduce-scatter.46.cloned.1.call-done = bf16[160,1280]{1,0:T(8,128)(2,1)} async-done(((bf16[1280,1280]{1,0:T(8,128)(2,1)}), bf16[160,1280]{1,0:T(8,128)(2,1)}) %reduce-scatter.46.cloned.1.call-update) | async-done | bytes 409616 | tf_op jit(solution)/shard_map/reduce_scatter | solution.py:290
  1129.0 36.7 %reduce-scatter.44.cloned.1.call-done = bf16[320,160]{0,1:T(8,128)(2,1)} async-done(((bf16[320,1280]{0,1:T(8,128)(2,1)}), bf16[320,160]{0,1:T(8,128)(2,1)}) %reduce-scatter.44.cloned.1.call-update) | async-done | bytes 102416 | tf_op jit(solution)/shard_map/reduce_scatter | solution.py:290
  1167.3 37.6 %reduce-scatter.38.cloned.1.call-done = bf16[160,320]{1,0:T(8,128)(2,1)} async-done(((bf16[1280,320]{1,0:T(8,128)(2,1)}), bf16[160,320]{1,0:T(8,128)(2,1)}) %reduce-scatter.38.cloned.1.call-update) | async-done | bytes 102416 | tf_op jit(solution)/shard_map/reduce_scatter | solution.py:290
  1206.6 61.5 %all-reduce = (f32[1280]{0:T(1024)S(1)}, f32[1280]{0:T(1024)S(1)}, f32[1280]{0:T(1024)S(1)}, f32[5120]{0:T(1024)S(1)}, f32[5120]{0:T(1024)S(1)}) all-reduce(f32[1280]{0:T(1024)S(1)} %add.338, f32[1280]{0:T(1024)S(1)} %add.339, f32[1280]{0:T(1024)S(1)} %add_dynamic-update-slice_fusion.1, ...), channel_id=1, replica_groups=mesh['shard'=2,'ctx'=4,'tp'=4] {'ctx','tp'}, use_global_device_ids=true, to_apply=%region_57.58 | all-reduce | flops 14080 | bytes 112640 | tf_op jit(solution)/shard_map/psum | solution.py:317
  1268.1 8.6 all-reduce.1
  1285.0 36.9 %reduce-scatter.36.cloned.1.call-done = bf16[160,1280]{1,0:T(8,128)(2,1)} async-done(((bf16[640,1280]{1,0:T(8,128)(2,1)}), bf16[160,1280]{1,0:T(8,128)(2,1)}) %reduce-scatter.36.cloned.1.call-update) | async-done | bytes 409616 | tf_op jit(solution)/shard_map/reduce_scatter | solution.py:71
  1321.9 38.3 %reduce-scatter.32.cloned.1.call-done = bf16[160,1280]{1,0:T(8,128)(2,1)} async-done(((bf16[640,1280]{1,0:T(8,128)(2,1)}), bf16[160,1280]{1,0:T(8,128)(2,1)}) %reduce-scatter.32.cloned.1.call-update) | async-done | bytes 409616 | tf_op jit(solution)/shard_map/reduce_scatter | solution.py:71
  (633 shorter events, 458.6 us)
Async XLA Ops:
  8.0 43.9 %all-gather.40.cloned.1.call-start = ((), (), s32[]{:S(2)}) async-start(), calls=%async_computation.44 | async-start | bytes 2048000 | tf_op jit(solution)/shard_map/all_gather | solution.py:59
  10.2 80.9 %all-gather.38.cloned.1.call-start = ((), (), s32[]{:S(2)}) async-start(), calls=%async_computation.43 | async-start | bytes 2048000 | tf_op jit(solution)/shard_map/all_gather | solution.py:59
  11.0 128.2 %all-gather.16.cloned.1.call-start = ((), (), s32[]{:S(2)}) async-start(), calls=%async_computation.17 | async-start | bytes 4096000 | tf_op jit(solution)/shard_map/all_gather | solution.py:112
  35.4 62.4 %copy-start.9 = (bf16[1280,320]{1,0:T(8,128)(2,1)}, bf16[1280,320]{1,0:T(8,128)(2,1)S(1)}, u32[]{:S(2)}) copy-start(bf16[1280,320]{1,0:T(8,128)(2,1)S(1)} %all_gather.53) | copy-start | bytes 2457604
  54.5 48.1 %copy-start.15 = (f32[640,320]{0,1:T(8,128)}, f32[640,320]{0,1:T(8,128)S(1)}, u32[]{:S(2)}) copy-start(f32[640,320]{0,1:T(8,128)S(1)} %fusion.165) | copy-start | bytes 2457604
  54.6 39.2 %copy-start.83 = (f32[640,5]{0,1:T(8,128)}, f32[640,5]{0,1:T(8,128)S(1)}, u32[]{:S(2)}) copy-start(f32[640,5]{0,1:T(8,128)S(1)} %multiply_reduce_fusion.18) | copy-start | bytes 38404
  54.6 48.0 %copy-start.73 = (f32[640,5]{0,1:T(8,128)}, f32[640,5]{0,1:T(8,128)S(1)}, u32[]{:S(2)}) copy-start(f32[640,5]{0,1:T(8,128)S(1)} %add_rsqrt_fusion.1) | copy-start | bytes 38404
  108.4 138.3 %reduce-scatter.22.cloned.1.call-start = ((), (), s32[]{:S(2)}) async-start(), calls=%async_computation.18 | async-start | bytes 2048000 | tf_op jit(solution)/shard_map/reduce_scatter | solution.py:71
  150.4 57.9 %copy-start.66 = (bf16[320,1280]{0,1:T(8,128)(2,1)S(1)}, bf16[320,1280]{0,1:T(8,128)(2,1)}, u32[]{:S(2)}) copy-start(bf16[320,1280]{0,1:T(8,128)(2,1)} %all_gather.56) | copy-start | bytes 2457604
  208.3 44.4 %copy-start.2 = (pred[640,2560]{1,0:T(32,128)(4,1)}, pred[640,2560]{1,0:T(32,128)(4,1)S(1)}, u32[]{:S(2)}) copy-start(pred[640,2560]{1,0:T(32,128)(4,1)S(1)} %get-tuple-element.786) | copy-start | bytes 4915204
  208.3 40.2 %copy-start.8 = (bf16[2,1,160,1280]{3,2,1,0:T(8,128)(2,1)S(1)}, bf16[2,1,160,1280]{3,2,1,0:T(8,128)(2,1)}, u32[]{:S(2)}) copy-start(bf16[2,1,160,1280]{3,2,1,0:T(8,128)(2,1)} %param.24) | copy-start | bytes 2457604
  208.3 40.2 %copy-start.68 = (f32[1280]{0:T(1024)S(1)}, f32[1280]{0:T(1024)}, u32[]{:S(2)}) copy-start(f32[1280]{0:T(1024)} %param.34) | copy-start | bytes 15364
  211.9 42.1 %copy-start.29 = (bf16[1280,320]{1,0:T(8,128)(2,1)S(1)}, bf16[1280,320]{1,0:T(8,128)(2,1)}, u32[]{:S(2)}) copy-start(bf16[1280,320]{1,0:T(8,128)(2,1)} %all_gather.54) | copy-start | bytes 2457604
  211.9 45.5 %all-gather.22.cloned.1.call-start = ((), (), s32[]{:S(2)}) async-start(), calls=%async_computation.21 | async-start | bytes 3686400 | tf_op jit(solution)/shard_map/all_gather | solution.py:263
  212.5 77.3 %all-gather.18.cloned.1.call-start = ((), (), s32[]{:S(2)}) async-start(), calls=%async_computation.19 | async-start | bytes 2048000 | tf_op jit(solution)/shard_map/all_gather | solution.py:59
  252.7 70.6 %all-gather.20.cloned.1.call-start = ((), (), s32[]{:S(2)}) async-start(), calls=%async_computation.20 | async-start | bytes 3686400 | tf_op jit(solution)/shard_map/all_gather | solution.py:262
  253.3 104.8 %all-gather.24.cloned.1.call-start = ((), (), s32[]{:S(2)}) async-start(), calls=%async_computation.22 | async-start | bytes 3686400 | tf_op jit(solution)/shard_map/all_gather | solution.py:264
  254.0 134.9 %all-gather.26.cloned.1.call-start = ((), (), s32[]{:S(2)}) async-start(), calls=%async_computation.24 | async-start | bytes 4096000 | tf_op jit(solution)/shard_map/all_gather | solution.py:112
  257.3 144.4 %reduce-scatter.24.cloned.1.call-start = ((), (), s32[]{:S(2)}) async-start(), calls=%async_computation.23 | async-start | bytes 2048000 | tf_op jit(solution)/shard_map/reduce_scatter | solution.py:71
  257.4 65.9 %copy-start.118 = (f32[1280]{0:T(1024)S(1)}, f32[1280]{0:T(1024)}, u32[]{:S(2)}) copy-start(f32[1280]{0:T(1024)} %param.37) | copy-start | bytes 15364
  364.0 101.3 %all-gather.30.cloned.1.call-start = ((), (), s32[]{:S(2)}) async-start(), calls=%async_computation.28 | async-start | bytes 2048000 | tf_op jit(solution)/shard_map/all_gather | solution.py:63
  409.0 92.4 %reduce-scatter.26.cloned.1.call-start = ((), (), s32[]{:S(2)}) async-start(), calls=%async_computation.25 | async-start | bytes 2048000 | tf_op jit(solution)/shard_map/reduce_scatter | solution.py:71
  465.0 74.1 %reduce-scatter.30.cloned.1.call-start = ((), (), s32[]{:S(2)}) async-start(), calls=%async_computation.29 | async-start | bytes 2048000 | tf_op jit(solution)/shard_map/reduce_scatter | solution.py:71
  480.2 58.9 %copy-start.23 = (f32[160,1280]{1,0:T(8,128)S(1)}, f32[160,1280]{1,0:T(8,128)}, u32[]{:S(2)}) copy-start(f32[160,1280]{1,0:T(8,128)} %copy-done.22) | copy-start | bytes 2457604
  483.7 96.4 %all-gather.28.cloned.1.call-start = ((), (), s32[]{:S(2)}) async-start(), calls=%async_computation.26 | async-start | bytes 2048000 | tf_op jit(solution)/shard_map/all_gather | solution.py:59
  501.4 40.4 %copy-start.12 = (bf16[160,1280]{1,0:T(8,128)(2,1)S(1)}, bf16[160,1280]{1,0:T(8,128)(2,1)}, u32[]{:S(2)}) copy-start(bf16[160,1280]{1,0:T(8,128)(2,1)} %reduce-scatter.26.cloned.1.call-done) | copy-start | bytes 1228804
  543.0 86.3 %reduce-scatter.28.cloned.1.call-start = ((), (), s32[]{:S(2)}) async-start(), calls=%async_computation.27 | async-start | bytes 2048000 | tf_op jit(solution)/shard_map/reduce_scatter | solution.py:71
  590.4 40.1 %copy-start.37 = (bf16[2,1,160,1280]{3,2,1,0:T(8,128)(2,1)S(1)}, bf16[2,1,160,1280]{3,2,1,0:T(8,128)(2,1)}, u32[]{:S(2)}) copy-start(bf16[2,1,160,1280]{3,2,1,0:T(8,128)(2,1)} %param.39) | copy-start | bytes 2457604
  593.9 78.7 %all-gather.34.cloned.1.call-start = ((), (), s32[]{:S(2)}) async-start(), calls=%async_computation.32 | async-start | bytes 2048000 | tf_op jit(solution)/shard_map/all_gather | solution.py:63
  635.5 90.2 %reduce-scatter.34.cloned.1.call-start = ((), (), s32[]{:S(2)}) async-start(), calls=%async_computation.33 | async-start | bytes 2048000 | tf_op jit(solution)/shard_map/reduce_scatter | solution.py:71
  686.9 38.9 %copy-start.62 = (bf16[160,1280]{1,0:T(8,128)(2,1)S(1)}, bf16[160,1280]{1,0:T(8,128)(2,1)}, u32[]{:S(2)}) copy-start(bf16[160,1280]{1,0:T(8,128)(2,1)} %reduce-scatter.30.cloned.1.call-done) | copy-start | bytes 1228804
  690.4 78.2 %all-gather.32.cloned.1.call-start = ((), (), s32[]{:S(2)}) async-start(), calls=%async_computation.30 | async-start | bytes 2048000 | tf_op jit(solution)/shard_map/all_gather | solution.py:63
  731.5 121.9 %all-gather.36.cloned.1.call-start = ((), (), s32[]{:S(2)}) async-start(), calls=%async_computation.34 | async-start | bytes 2048000 | tf_op jit(solution)/shard_map/all_gather | solution.py:63
  733.7 245.9 %reduce-scatter.52.cloned.1.call-start = ((), (), s32[]{:S(2)}) async-start(), calls=%async_computation.45 | async-start | bytes 4096000
  853.1 128.8 %reduce-scatter.54.cloned.1.call-start = ((), (), s32[]{:S(2)}) async-start(), calls=%async_computation.46 | async-start | bytes 4096000
  938.4 88.1 %reduce-scatter.50.cloned.1.call-start = ((), (), s32[]{:S(2)}) async-start(), calls=%async_computation.42 | async-start | bytes 3686400 | tf_op jit(solution)/shard_map/reduce_scatter | solution.py:290
  948.2 128.5 %reduce-scatter.48.cloned.1.call-start = ((), (), s32[]{:S(2)}) async-start(), calls=%async_computation.41 | async-start | bytes 3686400 | tf_op jit(solution)/shard_map/reduce_scatter | solution.py:290
  958.9 168.0 %reduce-scatter.46.cloned.1.call-start = ((), (), s32[]{:S(2)}) async-start(), calls=%async_computation.40 | async-start | bytes 3686400 | tf_op jit(solution)/shard_map/reduce_scatter | solution.py:290
  968.8 197.0 %reduce-scatter.44.cloned.1.call-start = ((), (), s32[]{:S(2)}) async-start(), calls=%async_computation.39 | async-start | bytes 1105920 | tf_op jit(solution)/shard_map/reduce_scatter | solution.py:290
  974.1 230.8 %reduce-scatter.38.cloned.1.call-start = ((), (), s32[]{:S(2)}) async-start(), calls=%async_computation.36 | async-start | bytes 1105920 | tf_op jit(solution)/shard_map/reduce_scatter | solution.py:290
  979.0 299.7 %reduce-scatter.42.cloned.1.call-start = ((), (), s32[]{:S(2)}) async-start(), calls=%async_computation.38 | async-start | bytes 1105920 | tf_op jit(solution)/shard_map/reduce_scatter | solution.py:290
  990.2 293.2 %reduce-scatter.40.cloned.1.call-start = ((), (), s32[]{:S(2)}) async-start(), calls=%async_computation.37 | async-start | bytes 1105920 | tf_op jit(solution)/shard_map/reduce_scatter | solution.py:290
  1007.3 314.6 %reduce-scatter.36.cloned.1.call-start = ((), (), s32[]{:S(2)}) async-start(), calls=%async_computation.35 | async-start | bytes 2048000 | tf_op jit(solution)/shard_map/reduce_scatter | solution.py:71
  1012.4 347.9 %reduce-scatter.32.cloned.1.call-start = ((), (), s32[]{:S(2)}) async-start(), calls=%async_computation.31 | async-start | bytes 2048000 | tf_op jit(solution)/shard_map/reduce_scatter | solution.py:71
  1018.5 110.4 %copy-start.36 = (f32[640,320]{0,1:T(8,128)S(1)}, f32[640,320]{0,1:T(8,128)}, u32[]{:S(2)}) copy-start(f32[640,320]{0,1:T(8,128)} %get-tuple-element.392) | copy-start | bytes 2457604
  1019.8 340.4 %copy-start.32 = (f32[160,1280]{1,0:T(8,128)S(1)}, f32[160,1280]{1,0:T(8,128)}, u32[]{:S(2)}) copy-start(f32[160,1280]{1,0:T(8,128)} %get-tuple-element.337) | copy-start | bytes 2457604
  1019.8 340.4 %copy-start.34 = (f32[160,1280]{1,0:T(8,128)S(1)}, f32[160,1280]{1,0:T(8,128)}, u32[]{:S(2)}) copy-start(f32[160,1280]{1,0:T(8,128)} %copy-done.33) | copy-start | bytes 2457604
  1019.9 340.4 %copy-start.69 = (f32[1280]{0:T(1024)S(1)}, f32[1280]{0:T(1024)}, u32[]{:S(2)}) copy-start(f32[1280]{0:T(1024)} %param.34) | copy-start | bytes 15364
  (121 other events, 541.8 us)
Sparse Core Ops, SparseCore 0:
  11.0 40.8 all-gather.39
  54.0 37.0 all-gather.37
  108.5 30.6 all-gather.15
  212.0 34.6 reduce-scatter.21
  364.1 36.3 reduce-scatter.23
  409.1 38.1 all-gather.29
  465.1 36.2 reduce-scatter.25
  503.8 35.3 reduce-scatter.29
  594.1 35.1 reduce-scatter.27
  690.6 35.1 reduce-scatter.33
  853.2 37.6 reduce-scatter.51
  938.5 37.6 reduce-scatter.53
  979.6 46.8 reduce-scatter.49
  1029.8 46.8 reduce-scatter.47
  1080.0 46.8 reduce-scatter.45
  1129.9 35.7 reduce-scatter.43
  1169.1 35.7 reduce-scatter.37
  1208.0 35.7 reduce-scatter.41
  1247.3 36.0 reduce-scatter.39
  1285.6 36.2 reduce-scatter.35
  1324.9 35.3 reduce-scatter.31
Sparse Core Ops, SparseCore 1:
  214.4 31.0 all-gather.21
  252.7 37.0 all-gather.17
  291.7 31.5 all-gather.19
  325.4 32.7 all-gather.23
  359.7 29.1 all-gather.25
  543.1 37.0 all-gather.27
  635.6 37.0 all-gather.33
  731.5 37.0 all-gather.31
  770.1 36.8 all-gather.35
